TPU v7x, 32 devices: a whole 2x2x4 slice. The times are simulated.
32 devices in a mesh: grp: 2 (over y), trade: 4 (over z), date: 2 (over x), path: 2 (over core).
Axes of the slice: x: 2, y: 2, z: 4, core: 2. Of those that a mesh axis runs over, the one named last changes fastest.
Arguments:
- driver_increments: float32 [16, 256, 128], P(('grp', 'date'), 'path'), parts along dimension 0, may hold values from -4 to 4
- persistence_ratio: float32 [16, 128], P(('grp', 'date')), parts along dimension 0, may hold values from 0 to 1, as said below
- deal_sensitivity: bfloat16 [128, 65536], P(None, ('grp', 'trade')), parts along dimension 1, may hold values from -0.5 to 0.5
- signed_notional: float32 [65536], P(('grp', 'trade')), parts along dimension 0, may hold values from -0.4 to 0.4
- batch_obligor: int32 [512], P(('grp', 'trade')), parts along dimension 0, may hold values from 0 to 127, as said below
- collateral_ceiling: float32 [256], P(('grp', 'trade')), parts along dimension 0, may hold values from -1 to 1
- default_discount_mass: float32 [16, 128], P(('grp', 'date'), 'trade'), parts along dimension 0, may hold values from 0.1 to 1
Outputs:
- exposure_profile: float32 [16, 128], P(('grp', 'date'), 'trade'), parts along dimension 0
- shock_gradient: float32 [16, 256, 128], P(('grp', 'date'), 'path'), parts along dimension 0
There are 2 independent parts, one for each index of `grp`. A program takes and returns all parts, laid end to end along the dimension named above; each array names one. Nothing has to cross between parts.
Inputs may be any that keep to these rules, and one draw needn't show every extreme that they name: `persistence_ratio`: strictly between 0 and 1. `batch_obligor`: counterparty c belongs to trade shard c // 32. Of the 64 trade blocks of one trade shard, at most 32 have counterparties on any one trade shard, and in every trade shard some counterparty shard receives exactly 32 of them.
All inputs are finite; a program needn't handle non-finite values.
Results may differ from a plain program's by a relative error of at most 0.0019.
Values sent between devices are 32-bit elements; how exact they have to be, the bound alone decides.
No kernel may reach another device: no remote copies, remote signals or barrier semaphores. Data moves between devices by JAX's collectives and lax.ppermute only.
A program may use at most 64 MiB of HBM per device.

v0:
```python
import jax
import jax.numpy as jnp
from jax import lax
from jax.sharding import PartitionSpec as P

block_width = 128
cluster_extent = 512
highest = lax.Precision.HIGHEST


def entering(value, axis, combine, identity, reverse):
    length, index = (lax.axis_size(axis), lax.axis_index(axis))
    everything = jax.tree.map(lambda part: lax.all_gather(part, axis), value)
    start = jax.tree.map(
        lambda part, zero: jnp.broadcast_to(jnp.asarray(zero, part.dtype), part.shape),
        value,
        identity,
    )

    def hop(k, before):
        at = length - 1 - k if reverse else k
        reached = at > index if reverse else at < index
        new = combine(before, jax.tree.map(lambda part: part[at], everything))
        return jax.tree.map(lambda a, b: jnp.where(reached, a, b), new, before)

    return lax.fori_loop(0, length, hop, start)


def compose(earlier, later):
    return (later[0] * earlier[0], later[0] * earlier[1] + later[1])


def reverse_chain(direct, persistence_ratio):
    date_count = direct.shape[0]
    factor_gain = jnp.ones((direct.shape[2],), jnp.float32)
    message = jnp.zeros(direct.shape[1:], jnp.float32)
    for date_step in reversed(range(date_count)):
        message = persistence_ratio[date_step][None, :] * (direct[date_step] + message)
        factor_gain = persistence_ratio[date_step] * factor_gain
    identity = (jnp.ones_like(factor_gain), jnp.zeros_like(message))
    _, arriving = entering((factor_gain, message), "date", compose, identity, True)
    adjoints = []
    message = arriving
    for date_step in reversed(range(date_count)):
        adjoint = direct[date_step] + message
        adjoints.append(adjoint)
        message = persistence_ratio[date_step][None, :] * adjoint
    return jnp.stack(adjoints[::-1])


def shards(
    driver_increments,
    persistence_ratio,
    deal_sensitivity,
    signed_notional,
    batch_obligor,
    collateral_ceiling,
    default_discount_mass,
):
    date_count, path_count, factor_count = driver_increments.shape
    factor_gain = jnp.ones((factor_count,), jnp.float32)
    carried = jnp.zeros((path_count, factor_count), jnp.float32)
    for date_step in range(date_count):
        carried = persistence_ratio[date_step][None, :] * carried + driver_increments[date_step]
        factor_gain = persistence_ratio[date_step] * factor_gain
    identity = (jnp.ones_like(factor_gain), jnp.zeros_like(carried))
    _, arriving = entering((factor_gain, carried), "date", compose, identity, False)
    states = []
    carried = arriving
    for date_step in range(date_count):
        carried = persistence_ratio[date_step][None, :] * carried + driver_increments[date_step]
        states.append(carried)
    row_count = date_count * path_count
    state_bf = jnp.stack(states).reshape(row_count, factor_count).astype(jnp.bfloat16)
    deal_ordinal = deal_sensitivity.shape[1]
    block_count = deal_ordinal // block_width
    cluster_ordinal = deal_ordinal // cluster_extent
    per_group = cluster_extent // block_width

    def value_group(group_index, block_sums):
        opening_offset = group_index * cluster_extent
        sensitivity_portion = lax.dynamic_slice_in_dim(
            deal_sensitivity, opening_offset, cluster_extent, 1
        )
        size_part = lax.dynamic_slice_in_dim(signed_notional, opening_offset, cluster_extent, 0)
        linear = jnp.dot(state_bf, sensitivity_portion, preferred_element_type=jnp.float32)
        trade_value = jax.nn.softplus(linear) * size_part[None, :]
        summed = trade_value.reshape(row_count, per_group, block_width).sum(axis=2)
        return lax.dynamic_update_slice_in_dim(block_sums, summed.T, group_index * per_group, 0)

    block_sums = lax.fori_loop(
        0, cluster_ordinal, value_group, jnp.zeros((block_count, row_count), jnp.float32)
    )
    cpty_dev = collateral_ceiling.shape[0]
    shard_count = lax.axis_size("trade")
    ownership = (
        batch_obligor[:, None] == jnp.arange(cpty_dev * shard_count, dtype=jnp.int32)[None, :]
    ).astype(jnp.float32)
    partial_value = lax.dot_general(
        ownership, block_sums, (((0,), (0,)), ((), ())), precision=highest
    )
    netted = lax.psum_scatter(partial_value, "trade", scatter_dimension=0, tiled=True)
    shifted = netted - collateral_ceiling[:, None]
    exposure = jax.nn.softplus(shifted).reshape(cpty_dev, date_count, path_count)
    path_total = lax.psum(jnp.sum(exposure, axis=2).T, "path")
    exposure_profile = path_total / (path_count * lax.axis_size("path"))
    net_adjoint = (
        default_discount_mass.T[:, :, None]
        * jax.nn.sigmoid(shifted).reshape(cpty_dev, date_count, path_count)
    ).reshape(cpty_dev, row_count)
    gathered = lax.all_gather(net_adjoint, "trade", axis=0, tiled=True)
    block_adjoint = jnp.dot(ownership, gathered, precision=highest)

    def pull_group(group_index, running):
        opening_offset = group_index * cluster_extent
        sensitivity_portion = lax.dynamic_slice_in_dim(
            deal_sensitivity, opening_offset, cluster_extent, 1
        )
        size_part = lax.dynamic_slice_in_dim(signed_notional, opening_offset, cluster_extent, 0)
        linear = jnp.dot(state_bf, sensitivity_portion, preferred_element_type=jnp.float32)
        slope_term = jax.nn.sigmoid(linear) * size_part[None, :]
        upstream = lax.dynamic_slice_in_dim(block_adjoint, group_index * per_group, per_group, 0)
        value_adjoint = (
            (upstream.T[:, :, None] * slope_term.reshape(row_count, per_group, block_width))
            .reshape(row_count, cluster_extent)
            .astype(jnp.bfloat16)
        )
        product = lax.dot_general(
            value_adjoint,
            sensitivity_portion,
            (((1,), (1,)), ((), ())),
            preferred_element_type=jnp.float32,
        )
        return running + product

    direct = lax.fori_loop(
        0, cluster_ordinal, pull_group, jnp.zeros((row_count, factor_count), jnp.float32)
    )
    direct = direct.reshape(date_count, path_count, factor_count)
    summed = lax.psum(direct, "trade")
    shock_gradient = reverse_chain(summed, persistence_ratio)
    return (exposure_profile, shock_gradient)


def solution(mesh):
    return jax.shard_map(
        shards,
        mesh=mesh,
        in_specs=(
            P(("grp", "date"), "path", None),
            P(("grp", "date"), None),
            P(None, ("grp", "trade")),
            P(("grp", "trade")),
            P(("grp", "trade")),
            P(("grp", "trade")),
            P(("grp", "date"), "trade"),
        ),
        out_specs=(P(("grp", "date"), "trade"), P(("grp", "date"), "path", None)),
        check_vma=False,
    )
```

profile of v0, /device:TPU:0, one launch (start us, length us, event | category | flops | bytes accessed | tf_op | source)
XLA Modules:
  0.0 200.2 jit_solution(7079904627721618631)
XLA Ops:
  7.2 0.8 multiply_bitcast_fusion
  8.8 5.1 %all-gather = f32[2,1,128]{2,1,0:T(1,128)S(1)} all-gather(f32[1,1,128]{2,1,0:T(1,128)S(1)} %get-tuple-element.550), channel_id=1, replica_groups=mesh['grp'=2,'trade'=4,'date'=2,'path'=2] {'date'}, dimensions={0}, use_global_device_ids=true | all-gather | bytes 1536 | tf_op jit(solution)/shard_map/all_gather | solution.py:13
  13.8 1.0 multiply_add_fusion
  14.8 4.9 %all_gather.20 = f32[2,128,128]{2,1,0:T(8,128)S(1)} all-gather(f32[1,128,128]{2,1,0:T(8,128)S(1)} %multiply_add_fusion), channel_id=1, replica_groups=mesh['grp'=2,'trade'=4,'date'=2,'path'=2] {'date'}, dimensions={0}, use_global_device_ids=true | all-gather | bytes 196608 | tf_op jit(solution)/shard_map/all_gather | solution.py:13
  19.9 0.9 convert_bitcast_fusion.1
  20.9 41.0 %while.57 = (s32[]{:T(128)}, f32[64,512]{1,0:T(8,128)S(1)}, bf16[128,8192]{1,0:T(8,128)(2,1)}, bf16[512,128]{1,0:T(8,128)(2,1)S(1)}, f32[8192]{0:T(1024)}, /*ind...) while((s32[]{:T(128)}, f32[64,512]{1,0:T(8,128)S(1)}, ...), condition=%wide.region_4.5_spmd, body=%wide.region_2.4_spmd.sunk | while | flops 69203976 | bytes 293085 | solution.py:91
  20.9 0.8 dynamic_slice.97
  21.7 1.8 bitcast_reduce_fusion.2
  23.5 0.8 dynamic_slice.97
  24.2 1.8 bitcast_reduce_fusion.2
  26.0 0.8 dynamic_slice.97
  26.8 1.8 bitcast_reduce_fusion.2
  28.6 0.8 dynamic_slice.97
  29.4 1.8 bitcast_reduce_fusion.2
  31.1 0.8 dynamic_slice.97
  31.9 1.8 bitcast_reduce_fusion.2
  33.7 0.8 dynamic_slice.97
  34.5 1.8 bitcast_reduce_fusion.2
  36.3 0.8 dynamic_slice.97
  37.0 1.8 bitcast_reduce_fusion.2
  38.8 0.8 dynamic_slice.97
  39.6 1.7 bitcast_reduce_fusion.2
  41.4 0.8 dynamic_slice.97
  42.2 1.8 bitcast_reduce_fusion.2
  43.9 0.8 dynamic_slice.97
  44.7 1.8 bitcast_reduce_fusion.2
  46.5 0.8 dynamic_slice.97
  47.3 1.8 bitcast_reduce_fusion.2
  49.1 0.8 dynamic_slice.97
  49.8 1.7 bitcast_reduce_fusion.2
  52.4 1.8 bitcast_reduce_fusion.2
  55.0 1.8 bitcast_reduce_fusion.2
  56.8 0.8 dynamic_slice.97
  57.5 1.8 bitcast_reduce_fusion.2
  60.1 1.8 bitcast_reduce_fusion.2
  61.9 1.1 fusion.27
  63.1 21.4 %reduce-scatter.2.cloned.1.call-done = f32[32,512]{1,0:T(8,128)} async-done(((f32[128,512]{1,0:T(8,128)}), f32[32,512]{1,0:T(8,128)}) %reduce-scatter.2.cloned.1.call-update) | async-done | bytes 65552 | tf_op jit(solution)/shard_map/reduce_scatter | solution.py:102
  84.6 1.0 bitcast_multiply_fusion
  85.6 13.8 %all_gather.21 = f32[128,512]{1,0:T(8,128)S(1)} all-gather(f32[32,512]{1,0:T(8,128)S(1)} %get-tuple-element.544), channel_id=1, replica_groups=mesh['grp'=2,'trade'=4,'date'=2,'path'=2] {'trade'}, dimensions={0}, use_global_device_ids=true | all-gather | bytes 327680 | tf_op jit(solution)/shard_map/all_gather | solution.py:111
  99.7 50.3 %while.59 = (s32[]{:T(128)}, f32[512,128]{1,0:T(8,128)S(1)}, f32[64,512]{1,0:T(8,128)S(1)}, bf16[128,8192]{1,0:T(8,128)(2,1)}, bf16[512,128]{1,0:T(8,128)(2,1)S(...) while((s32[]{:T(128)}, f32[512,128]{1,0:T(8,128)S(1)}, ...), condition=%wide.region_9.10_spmd.clone, body=%wide.region_8.9_spmd.clone.sunk | while | flops 135921680 | bytes 3063530 | solution.py:136
  101.3 1.6 fusion.50
  104.4 1.6 fusion.50
  107.6 1.6 fusion.50
  110.7 1.6 fusion.50
  113.8 1.6 fusion.50
  117.0 1.6 fusion.50
  120.1 1.6 fusion.50
  123.3 1.6 fusion.50
  126.4 1.6 fusion.50
  129.5 1.6 fusion.50
  132.7 1.6 fusion.50
  135.8 1.6 fusion.50
  139.0 1.6 fusion.50
  142.1 1.6 fusion.50
  145.3 1.6 fusion.50
  147.7 0.8 dynamic_slice.103
  148.4 1.6 fusion.50
  150.8 4.2 %all-gather.1 = f32[2,1,128]{2,1,0:T(1,128)S(1)} all-gather(f32[1,1,128]{2,1,0:T(1,128)S(1)} %get-tuple-element.546), channel_id=1, replica_groups=mesh['grp'=2,'trade'=4,'date'=2,'path'=2] {'date'}, dimensions={0}, use_global_device_ids=true | all-gather | bytes 1536 | tf_op jit(solution)/shard_map/all_gather | solution.py:13
  155.1 3.4 %psum.14 = f32[4,32]{0,1:T(8,128)S(1)} all-reduce(f32[4,32]{0,1:T(8,128)S(1)} %bitcast.153), channel_id=1, replica_groups=mesh['grp'=2,'trade'=4,'date'=2,'path'=2] {'path'}, use_global_device_ids=true, to_apply=%region_7.8 | all-reduce | flops 128 | bytes 1024 | tf_op jit(solution)/shard_map/psum | solution.py:105
  159.1 25.7 %all-reduce.2.cloned.1.call-done = f32[4,128,128]{2,1,0:T(8,128)} async-done(((f32[4,128,128]{2,1,0:T(8,128)}), f32[4,128,128]{2,1,0:T(8,128)}) %all-reduce.2.cloned.1.call-update) | async-done | bytes 262160 | tf_op jit(solution)/shard_map/psum | solution.py:140
  184.8 1.0 add_multiply_fusion
  185.8 4.9 %all_gather.23 = f32[2,128,128]{2,1,0:T(8,128)S(1)} all-gather(f32[1,128,128]{2,1,0:T(8,128)S(1)} %add_multiply_fusion), channel_id=1, replica_groups=mesh['grp'=2,'trade'=4,'date'=2,'path'=2] {'date'}, dimensions={0}, use_global_device_ids=true | all-gather | bytes 196608 | tf_op jit(solution)/shard_map/all_gather | solution.py:13
  190.8 1.0 fusion.23
  191.8 0.9 fusion.29
  (121 shorter events, 30.0 us)
Async XLA Ops:
  7.2 13.6 %copy-start = (f32[4,128,128]{2,1,0:T(8,128)S(1)}, f32[4,128,128]{2,1,0:T(8,128)}, u32[]{:S(2)}) copy-start(f32[4,128,128]{2,1,0:T(8,128)} %param.15) | copy-start | bytes 786436
  7.2 77.3 %reduce-scatter.2.cloned.1.call-start = ((), (), s32[]{:S(2)}) async-start(), calls=%async_computation.1 | async-start | bytes 327680 | tf_op jit(solution)/shard_map/reduce_scatter | solution.py:102
  20.8 41.0 %copy-start.2 = (s32[64]{0:T(128)S(1)}, s32[64]{0:T(128)}, u32[]{:S(2)}) copy-start(s32[64]{0:T(128)} %param.19) | copy-start | bytes 772
  20.9 42.2 %copy-start.3 = (f32[4,32]{1,0:T(4,128)S(1)}, f32[4,32]{1,0:T(4,128)}, u32[]{:S(2)}) copy-start(f32[4,32]{1,0:T(4,128)} %param.21) | copy-start | bytes 1540
  20.9 63.7 %copy-start.4 = (f32[32]{0:T(128)S(1)}, f32[32]{0:T(128)}, u32[]{:S(2)}) copy-start(f32[32]{0:T(128)} %param.20) | copy-start | bytes 388
  63.0 121.9 %all-reduce.2.cloned.1.call-start = ((), (), s32[]{:S(2)}) async-start(), calls=%async_computation.2 | async-start | bytes 524288 | tf_op jit(solution)/shard_map/psum | solution.py:140
  150.0 0.7 copy-start.1
Sparse Core Ops, SparseCore 0:
  63.1 21.3 reduce-scatter.1
  150.9 33.9 all-reduce.1
where the time goes:
time: 202 us; the launch traced here: 200 us
  matrix products  54.4 us (27%)
  waiting for transfers between devices  47.1 us (23%)
  local copies, waits for them, and re-layouts  38.5 us (19%)
  blocking collectives  36.4 us (18%)
  between operations  14.2 us (7%)
  other arithmetic  8.08 us (4%)
    dot_general x16, matrix products, value_group(): jnp.dot(state_bf, sensitivity_portion, preferred_element_type=jnp.float32)  28 us
    psum x1, waiting for transfers between devices, shards(): summed = lax.psum(direct, 'trade')  25.7 us
    dot_general x16, matrix products, pull_group(): lax.dot_general(value_adjoint, sensitivity_portion, (((1,), (1,)), ((), (...  25.1 us
    reduce_scatter x1, waiting for transfers between devices, shards(): lax.psum_scatter(partial_value, 'trade', scatter_dimension=0, tiled=True)  21.4 us
    all_gather x4, blocking collectives, entering(): everything = jax.tree.map(lambda part: lax.all_gather(part, axis), value)  19.2 us
    all_gather x1, blocking collectives, shards(): gathered = lax.all_gather(net_adjoint, 'trade', axis=0, tiled=True)  13.8 us
    dynamic_slice x16, local copies, waits for them, and re-layouts, value_group(): lax.dynamic_slice_in_dim(signed_notional, opening_offset, cluster_extent, 0)  12.2 us
    dynamic_slice x16, local copies, waits for them, and re-layouts, pull_group(): lax.dynamic_slice_in_dim(signed_notional, opening_offset, cluster_extent, 0)  12.2 us
  transfers between devices with their start and end apart: 2, of which 2 were waited for; matrix products, arithmetic and copies ran while one was open for 0% of the time, Pallas kernels for 0%

commit v1 on v0

--- a/solution.py
+++ b/solution.py
@@ -137,7 +137,8 @@
         0, cluster_ordinal, pull_group, jnp.zeros((row_count, factor_count), jnp.float32)
     )
     direct = direct.reshape(date_count, path_count, factor_count)
-    summed = lax.psum(direct, "trade")
+    parts = lax.all_gather(direct, "trade", axis=0, tiled=False)
+    summed = parts.sum(axis=0)
     shock_gradient = reverse_chain(summed, persistence_ratio)
     return (exposure_profile, shock_gradient)
 

time: 202 us -> 193 us (0.955)
  waiting for transfers between devices: 47.1 us -> 39.7 us
    psum x1 -> x0, waiting for transfers between devices: 25.7 us -> none  [shards(): summed = lax.psum(direct, 'trade')]
    all_gather x0 -> x1, waiting for transfers between devices: none -> 18.3 us  [shards(): parts = lax.all_gather(direct, 'trade', axis=0, tiled=False)]
where the time goes in v1:
time: 193 us; the launch traced here: 191 us
  matrix products  54.4 us (28%)
  waiting for transfers between devices  39.7 us (21%)
  local copies, waits for them, and re-layouts  38.5 us (20%)
  blocking collectives  36.4 us (19%)
  between operations  14.2 us (7%)
  other arithmetic  6.68 us (3%)
    dot_general x16, matrix products, value_group(): jnp.dot(state_bf, sensitivity_portion, preferred_element_type=jnp.float32)  28 us
    dot_general x16, matrix products, pull_group(): lax.dot_general(value_adjoint, sensitivity_portion, (((1,), (1,)), ((), (...  25.1 us
    reduce_scatter x1, waiting for transfers between devices, shards(): lax.psum_scatter(partial_value, 'trade', scatter_dimension=0, tiled=True)  21.4 us
    all_gather x4, blocking collectives, entering(): everything = jax.tree.map(lambda part: lax.all_gather(part, axis), value)  19.2 us
    all_gather x1, waiting for transfers between devices, shards(): parts = lax.all_gather(direct, 'trade', axis=0, tiled=False)  18.3 us
    all_gather x1, blocking collectives, shards(): gathered = lax.all_gather(net_adjoint, 'trade', axis=0, tiled=True)  13.8 us
    dynamic_slice x16, local copies, waits for them, and re-layouts, value_group(): lax.dynamic_slice_in_dim(signed_notional, opening_offset, cluster_extent, 0)  12.2 us
    dynamic_slice x16, local copies, waits for them, and re-layouts, pull_group(): lax.dynamic_slice_in_dim(signed_notional, opening_offset, cluster_extent, 0)  12.2 us
  transfers between devices with their start and end apart: 2, of which 2 were waited for; matrix products, arithmetic and copies ran while one was open for 0% of the time, Pallas kernels for 0%

profile of v1, /device:TPU:0, one launch (start us, length us, event | category | flops | bytes accessed | tf_op | source)
XLA Modules:
  0.0 191.5 jit_solution(786265495929406652)
XLA Ops:
  7.2 0.8 multiply_bitcast_fusion
  8.8 5.1 %all-gather = f32[2,1,128]{2,1,0:T(1,128)S(1)} all-gather(f32[1,1,128]{2,1,0:T(1,128)S(1)} %get-tuple-element.550), channel_id=1, replica_groups=mesh['grp'=2,'trade'=4,'date'=2,'path'=2] {'date'}, dimensions={0}, use_global_device_ids=true | all-gather | bytes 1536 | tf_op jit(solution)/shard_map/all_gather | solution.py:13
  13.8 1.0 multiply_add_fusion
  14.8 4.9 %all_gather.23 = f32[2,128,128]{2,1,0:T(8,128)S(1)} all-gather(f32[1,128,128]{2,1,0:T(8,128)S(1)} %multiply_add_fusion), channel_id=1, replica_groups=mesh['grp'=2,'trade'=4,'date'=2,'path'=2] {'date'}, dimensions={0}, use_global_device_ids=true | all-gather | bytes 196608 | tf_op jit(solution)/shard_map/all_gather | solution.py:13
  19.9 0.9 convert_bitcast_fusion.1
  20.9 41.0 %while.57 = (s32[]{:T(128)}, f32[64,512]{1,0:T(8,128)S(1)}, bf16[128,8192]{1,0:T(8,128)(2,1)}, bf16[512,128]{1,0:T(8,128)(2,1)S(1)}, f32[8192]{0:T(1024)}, /*ind...) while((s32[]{:T(128)}, f32[64,512]{1,0:T(8,128)S(1)}, ...), condition=%wide.region_4.5_spmd, body=%wide.region_2.4_spmd.sunk | while | flops 69203976 | bytes 293085 | solution.py:91
  20.9 0.8 dynamic_slice.97
  21.7 1.8 bitcast_reduce_fusion.2
  23.5 0.8 dynamic_slice.97
  24.2 1.8 bitcast_reduce_fusion.2
  26.0 0.8 dynamic_slice.97
  26.8 1.8 bitcast_reduce_fusion.2
  28.6 0.8 dynamic_slice.97
  29.4 1.8 bitcast_reduce_fusion.2
  31.1 0.8 dynamic_slice.97
  31.9 1.8 bitcast_reduce_fusion.2
  33.7 0.8 dynamic_slice.97
  34.5 1.8 bitcast_reduce_fusion.2
  36.3 0.8 dynamic_slice.97
  37.0 1.8 bitcast_reduce_fusion.2
  38.8 0.8 dynamic_slice.97
  39.6 1.7 bitcast_reduce_fusion.2
  41.4 0.8 dynamic_slice.97
  42.2 1.8 bitcast_reduce_fusion.2
  43.9 0.8 dynamic_slice.97
  44.7 1.8 bitcast_reduce_fusion.2
  46.5 0.8 dynamic_slice.97
  47.3 1.8 bitcast_reduce_fusion.2
  49.1 0.8 dynamic_slice.97
  49.8 1.7 bitcast_reduce_fusion.2
  51.6 0.8 dynamic_slice.97
  52.4 1.8 bitcast_reduce_fusion.2
  54.2 0.8 dynamic_slice.97
  55.0 1.8 bitcast_reduce_fusion.2
  56.8 0.8 dynamic_slice.97
  57.5 1.8 bitcast_reduce_fusion.2
  60.1 1.8 bitcast_reduce_fusion.2
  61.9 1.1 fusion.27
  63.1 21.4 %reduce-scatter.2.cloned.1.call-done = f32[32,512]{1,0:T(8,128)} async-done(((f32[128,512]{1,0:T(8,128)}), f32[32,512]{1,0:T(8,128)}) %reduce-scatter.2.cloned.1.call-update) | async-done | bytes 65552 | tf_op jit(solution)/shard_map/reduce_scatter | solution.py:102
  84.6 1.0 bitcast_multiply_fusion
  85.6 13.8 %all_gather.24 = f32[128,512]{1,0:T(8,128)S(1)} all-gather(f32[32,512]{1,0:T(8,128)S(1)} %get-tuple-element.544), channel_id=1, replica_groups=mesh['grp'=2,'trade'=4,'date'=2,'path'=2] {'trade'}, dimensions={0}, use_global_device_ids=true | all-gather | bytes 327680 | tf_op jit(solution)/shard_map/all_gather | solution.py:111
  99.7 50.3 %while.59 = (s32[]{:T(128)}, f32[512,128]{1,0:T(8,128)S(1)}, f32[64,512]{1,0:T(8,128)S(1)}, bf16[128,8192]{1,0:T(8,128)(2,1)}, bf16[512,128]{1,0:T(8,128)(2,1)S(...) while((s32[]{:T(128)}, f32[512,128]{1,0:T(8,128)S(1)}, ...), condition=%wide.region_9.10_spmd.clone, body=%wide.region_8.9_spmd.clone.sunk | while | flops 135921680 | bytes 3063530 | solution.py:136
  101.3 1.6 fusion.50
  104.4 1.6 fusion.50
  107.6 1.6 fusion.50
  110.7 1.6 fusion.50
  113.8 1.6 fusion.50
  117.0 1.6 fusion.50
  120.1 1.6 fusion.50
  123.3 1.6 fusion.50
  126.4 1.6 fusion.50
  129.5 1.6 fusion.50
  132.7 1.6 fusion.50
  135.8 1.6 fusion.50
  139.0 1.6 fusion.50
  142.1 1.6 fusion.50
  145.3 1.6 fusion.50
  147.7 0.8 dynamic_slice.103
  148.4 1.6 fusion.50
  150.8 4.2 %all-gather.1 = f32[2,1,128]{2,1,0:T(1,128)S(1)} all-gather(f32[1,1,128]{2,1,0:T(1,128)S(1)} %get-tuple-element.546), channel_id=1, replica_groups=mesh['grp'=2,'trade'=4,'date'=2,'path'=2] {'date'}, dimensions={0}, use_global_device_ids=true | all-gather | bytes 1536 | tf_op jit(solution)/shard_map/all_gather | solution.py:13
  155.1 3.4 %psum.7 = f32[4,32]{0,1:T(8,128)S(1)} all-reduce(f32[4,32]{0,1:T(8,128)S(1)} %bitcast.153), channel_id=1, replica_groups=mesh['grp'=2,'trade'=4,'date'=2,'path'=2] {'path'}, use_global_device_ids=true, to_apply=%region_7.8 | all-reduce | flops 128 | bytes 1024 | tf_op jit(solution)/shard_map/psum | solution.py:105
  159.1 18.3 %all-gather.4.cloned.1.call-done = f32[4,4,128,128]{3,2,1,0:T(8,128)} async-done(((f32[1,4,128,128]{3,2,1,0:T(8,128)}), f32[4,4,128,128]{3,2,1,0:T(8,128)}) %all-gather.4.cloned.1.call-update) | async-done | bytes 1048592 | tf_op jit(solution)/shard_map/all_gather | solution.py:140
  177.5 1.3 reduce_sum.32
  178.8 4.9 %all_gather.27 = f32[2,128,128]{2,1,0:T(8,128)S(1)} all-gather(f32[1,128,128]{2,1,0:T(8,128)S(1)} %add_multiply_fusion), channel_id=1, replica_groups=mesh['grp'=2,'trade'=4,'date'=2,'path'=2] {'date'}, dimensions={0}, use_global_device_ids=true | all-gather | bytes 196608 | tf_op jit(solution)/shard_map/all_gather | solution.py:13
  (122 shorter events, 28.5 us)
Async XLA Ops:
  7.2 13.6 %copy-start = (f32[4,128,128]{2,1,0:T(8,128)S(1)}, f32[4,128,128]{2,1,0:T(8,128)}, u32[]{:S(2)}) copy-start(f32[4,128,128]{2,1,0:T(8,128)} %param.15) | copy-start | bytes 786436
  7.2 77.3 %reduce-scatter.2.cloned.1.call-start = ((), (), s32[]{:S(2)}) async-start(), calls=%async_computation.1 | async-start | bytes 327680 | tf_op jit(solution)/shard_map/reduce_scatter | solution.py:102
  20.8 41.0 %copy-start.2 = (s32[64]{0:T(128)S(1)}, s32[64]{0:T(128)}, u32[]{:S(2)}) copy-start(s32[64]{0:T(128)} %param.19) | copy-start | bytes 772
  20.9 42.2 %copy-start.3 = (f32[4,32]{1,0:T(4,128)S(1)}, f32[4,32]{1,0:T(4,128)}, u32[]{:S(2)}) copy-start(f32[4,32]{1,0:T(4,128)} %param.21) | copy-start | bytes 1540
  20.9 63.7 %copy-start.4 = (f32[32]{0:T(128)S(1)}, f32[32]{0:T(128)}, u32[]{:S(2)}) copy-start(f32[32]{0:T(128)} %param.20) | copy-start | bytes 388
  63.0 114.5 %all-gather.4.cloned.1.call-start = ((), (), s32[]{:S(2)}) async-start(), calls=%async_computation.2 | async-start | bytes 1310720 | tf_op jit(solution)/shard_map/all_gather | solution.py:140
  150.0 0.7 copy-start.1
Sparse Core Ops, SparseCore 0:
  63.1 21.3 reduce-scatter.1
  150.9 26.5 all-gather.3
